TPU v7x, 32 devices: a whole 2x2x4 slice. The times are simulated.
32 devices in a mesh: section: 2 (over y), fsdp: 4 (over x, core), replica: 4 (over z).
Axes of the slice: x: 2, y: 2, z: 4, core: 2. Of those that a mesh axis runs over, the one named last changes fastest.
Arguments:
- images: bfloat16 [4, 32, 14, 14, 512], P(None, ('fsdp', 'replica')), may hold values from -6 to 6
- cotangent: bfloat16 [4, 32, 14, 14, 512], P(None, ('fsdp', 'replica')), may hold values from -6 to 6
- counts: int32 [4, 16], P(None, ('fsdp', 'replica')), may hold values from 1 to 2, as said below
- regions: int32 [14, 14], replicated, may hold values from 0 to 8, as said below
- relpos: int32 [49, 49], replicated, may hold values from 0 to 168, as said below
- qkv_weight: bfloat16 [2, 512, 1536], P('section', 'fsdp'), may hold values from -0.25 to 0.25
- proj_weight: bfloat16 [2, 512, 512], P('section', 'fsdp'), may hold values from -1.5 to 1.5
- fc1_weight: bfloat16 [2, 512, 2048], P('section', 'fsdp'), may hold values from -0.25 to 0.25
- fc2_weight: bfloat16 [2, 2048, 512], P('section', 'fsdp'), may hold values from -0.125 to 0.125
- gains: bfloat16 [2, 2, 512], P('section', None, 'fsdp'), may hold values from 0.099609375 to 1.8984375
- biases: bfloat16 [2, 6, 512], P('section', None, 'fsdp'), may hold values from -3 to 3
- fc1_bias: bfloat16 [2, 2048], P('section', 'fsdp'), may hold values from -3 to 3
- rel_table: bfloat16 [2, 169, 16], P('section', None, 'fsdp'), may hold values from -5 to 5
Outputs:
- block_out: bfloat16 [2, 4, 32, 14, 14, 512], P('section', None, ('fsdp', 'replica'))
- input_grad: float32 [2, 4, 32, 14, 14, 512], P('section', None, ('fsdp', 'replica'))
- grad_qkv: float32 [2, 512, 1536], P('section', 'fsdp')
- grad_proj: float32 [2, 512, 512], P('section', 'fsdp')
- grad_fc1: float32 [2, 512, 2048], P('section', 'fsdp')
- grad_fc2: float32 [2, 2048, 512], P('section', 'fsdp')
- grad_gains: float32 [2, 2, 512], P('section', None, 'fsdp')
- grad_biases: float32 [2, 6, 512], P('section', None, 'fsdp')
- grad_fc1_bias: float32 [2, 2048], P('section', 'fsdp')
- grad_table: float32 [2, 169, 16], P('section', None, 'fsdp')
Inputs may be any that keep to these rules, and one draw needn't show every extreme that they name: `counts`: slots 0 to count - 1 of a device's 2 slots in a micro-batch are live; in every micro-batch some device has all 2 live. `regions`: region ids are constant on bands: id = 3 * band(row) + band(column) with the same two cut positions for rows and columns. `relpos`: pairs with the same relative offset share a row; every row is used.
All inputs are finite; a program needn't handle non-finite values.
Results may differ from a plain program's by a relative error of at most 0.019.
Values may be sent and summed in bfloat16 or wider, within the bound.
No kernel may reach another device: no remote copies, remote signals or barrier semaphores. Data moves between devices by JAX's collectives and lax.ppermute only.
A program may use at most 320 MiB of HBM per device.

v0:
```python
import jax
import jax.numpy as jnp
from jax import lax
from jax.sharding import PartitionSpec as P

DIM = 512
HEADS = 16
HEAD_DIM = 32
WIN = 7
SIDE = 14
SHIFT = 3
TABLE = 169


EPSILON = 1e-05
ROOT_HALF = 0.7071067811865476
INV_ROOT_TAU = 0.3989422804014327


def shifted(value, axis, by):
    length = lax.axis_size(axis)
    pairs = [(i, i + by) for i in range(length) if 0 <= i + by < length]
    return lax.ppermute(value, axis, pairs)


def layer_norm(values, gain, offset_row):
    center = values - jnp.mean(values, axis=-1, keepdims=True)
    spread = jnp.mean(center * center, axis=-1, keepdims=True)
    scaled = lax.rsqrt(spread + EPSILON)
    normed = center * scaled
    return (normed * gain + offset_row, normed, scaled)


def norm_backward(upstream, normed, scaled, gain):
    direct = upstream * gain
    return (
        direct
        - jnp.mean(direct, axis=-1, keepdims=True)
        - normed * jnp.mean(direct * normed, axis=-1, keepdims=True)
    ) * scaled


def gelu_value(before):
    return 0.5 * before * (1.0 + jax.scipy.special.erf(before * ROOT_HALF))


def gelu_slope(before):
    return 0.5 * (
        1.0 + jax.scipy.special.erf(before * ROOT_HALF)
    ) + before * INV_ROOT_TAU * jnp.exp(-0.5 * before * before)


def inner_rows(left, right):
    return lax.dot_general(
        left, right, (((0,), (0,)), ((), ())), preferred_element_type=jnp.float32
    )


def outer_cols(left, right):
    return lax.dot_general(
        left, right, (((1,), (1,)), ((), ())), preferred_element_type=jnp.float32
    )


def to_windows(image_rows, offset):
    rolled = jnp.roll(image_rows, (-offset, -offset), axis=(1, 2))
    count = image_rows.shape[0]
    parts = SIDE // WIN
    shaped = rolled.reshape(count, parts, WIN, parts, WIN, DIM).transpose(0, 1, 3, 2, 4, 5)
    return shaped.reshape(count * SIDE * SIDE, DIM)


def from_windows(window_rows, offset):
    count = window_rows.shape[0] // (SIDE * SIDE)
    parts = SIDE // WIN
    shaped = window_rows.reshape(count, parts, parts, WIN, WIN, DIM).transpose(0, 1, 3, 2, 4, 5)
    return jnp.roll(shaped.reshape(count, SIDE, SIDE, DIM), (offset, offset), axis=(1, 2))


def relation_onehot(relpos):
    flat = relpos.reshape(-1)
    return (flat[:, None] == jnp.arange(TABLE, dtype=jnp.int32)[None, :]).astype(jnp.float32)


def region_mask(regions, later):
    parts = SIDE // WIN
    tiles = (
        regions.reshape(parts, WIN, parts, WIN)
        .transpose(0, 2, 1, 3)
        .reshape(parts * parts, WIN * WIN)
    )
    differ = (tiles[:, :, None] != tiles[:, None, :]) & later
    return jnp.where(differ, jnp.float32(-100.0), jnp.float32(0.0))


def window_eye():
    count = (SIDE // WIN) ** 2
    return lax.broadcasted_iota(jnp.int32, (count, count), 0) == lax.broadcasted_iota(
        jnp.int32, (count, count), 1
    )


def attention_add(table, onehot, masking):
    lookup = jnp.dot(onehot, table.astype(jnp.float32), precision=lax.Precision.HIGHEST)
    lookup = lookup.reshape(WIN * WIN, WIN * WIN, HEADS).transpose(2, 0, 1)
    windowed = lookup[None] + masking[:, None]
    count = (SIDE // WIN) ** 2
    eye = window_eye()
    spread_add = jnp.where(
        eye[None, :, None, :, None],
        windowed.transpose(1, 0, 2, 3)[:, :, :, None, :],
        jnp.float32(0.0),
    )
    full_add = spread_add.reshape(HEADS, count * WIN * WIN, count * WIN * WIN)
    same = jnp.broadcast_to(eye[:, None, :, None], (count, WIN * WIN, count, WIN * WIN)).reshape(
        count * WIN * WIN, count * WIN * WIN
    )
    return (full_add, same)


def forward(rows, params, added):
    qkv_w, proj_w, fc1_w, fc2_w, gain_rows, bias_rows, fc1_b, table = params
    full_add, same = added
    gains_f = gain_rows.astype(jnp.float32)
    biases_f = bias_rows.astype(jnp.float32)
    factor = HEAD_DIM ** (-0.5)
    base = rows.astype(jnp.float32)
    first, normed_a, scaled_a = layer_norm(base, gains_f[0], biases_f[0])
    first_b = first.astype(jnp.bfloat16)
    mixed = jnp.dot(first_b, qkv_w, preferred_element_type=jnp.float32)
    count = rows.shape[0] // (SIDE * SIDE)
    blocks = (count, SIDE * SIDE, HEADS, HEAD_DIM)
    query_blocks = ((mixed[:, :DIM] + biases_f[1]) * factor).astype(jnp.bfloat16).reshape(blocks)
    key_blocks = mixed[:, DIM : 2 * DIM].astype(jnp.bfloat16).reshape(blocks)
    value_blocks = (mixed[:, 2 * DIM :] + biases_f[2]).astype(jnp.bfloat16).reshape(blocks)
    scores = (
        jnp.einsum("sihd,sjhd->shij", query_blocks, key_blocks, preferred_element_type=jnp.float32)
        + full_add[None]
    )
    expo = jnp.where(same[None, None], jnp.exp(scores), jnp.float32(0.0))
    probs = expo / jnp.sum(expo, axis=-1, keepdims=True)
    probs_b = probs.astype(jnp.bfloat16)
    attended = jnp.einsum(
        "shij,sjhd->sihd", probs_b, value_blocks, preferred_element_type=jnp.float32
    )
    attended = attended.astype(jnp.bfloat16).reshape(rows.shape[0], DIM)
    middle = base + jnp.dot(attended, proj_w, preferred_element_type=jnp.float32) + biases_f[3]
    second, normed_b, scaled_b = layer_norm(middle, gains_f[1], biases_f[4])
    second_b = second.astype(jnp.bfloat16)
    before = jnp.dot(second_b, fc1_w, preferred_element_type=jnp.float32) + fc1_b.astype(
        jnp.float32
    )
    hidden_b = gelu_value(before).astype(jnp.bfloat16)
    output = middle + jnp.dot(hidden_b, fc2_w, preferred_element_type=jnp.float32) + biases_f[5]
    saved = (
        normed_a,
        scaled_a,
        first_b,
        query_blocks,
        key_blocks,
        value_blocks,
        probs,
        probs_b,
        attended,
        normed_b,
        scaled_b,
        second_b,
        before,
        hidden_b,
    )
    return (output.astype(jnp.bfloat16), saved)


def backward(upstream_rows, saved, params, onehot):
    qkv_w, proj_w, fc1_w, fc2_w, gain_rows, bias_rows, fc1_b, table = params
    gains_f = gain_rows.astype(jnp.float32)
    factor = HEAD_DIM ** (-0.5)
    (
        normed_a,
        scaled_a,
        first_b,
        query_blocks,
        key_blocks,
        value_blocks,
        probs,
        probs_b,
        attended,
        normed_b,
        scaled_b,
        second_b,
        before,
        hidden_b,
    ) = saved
    upstream = upstream_rows.astype(jnp.float32)
    grad_fc2_bias = jnp.sum(upstream, axis=0)
    grad_fc2 = inner_rows(hidden_b, upstream_rows)
    grad_before = outer_cols(upstream_rows, fc2_w) * gelu_slope(before)
    grad_before_b = grad_before.astype(jnp.bfloat16)
    grad_fc1_bias = jnp.sum(grad_before, axis=0)
    grad_fc1 = inner_rows(second_b, grad_before_b)
    grad_second = outer_cols(grad_before_b, fc1_w)
    grad_gain_b = jnp.sum(grad_second * normed_b, axis=0)
    grad_shift_b = jnp.sum(grad_second, axis=0)
    grad_middle = upstream + norm_backward(grad_second, normed_b, scaled_b, gains_f[1])
    grad_middle_b = grad_middle.astype(jnp.bfloat16)
    grad_proj_bias = jnp.sum(grad_middle, axis=0)
    grad_proj = inner_rows(attended, grad_middle_b)
    grad_attended = (
        outer_cols(grad_middle_b, proj_w).astype(jnp.bfloat16).reshape(query_blocks.shape)
    )
    grad_probs = jnp.einsum(
        "sihd,sjhd->shij", grad_attended, value_blocks, preferred_element_type=jnp.float32
    )
    grad_scores = probs * (grad_probs - jnp.sum(probs * grad_probs, axis=-1, keepdims=True))
    grad_scores_b = grad_scores.astype(jnp.bfloat16)
    count = (SIDE // WIN) ** 2
    summed = jnp.sum(grad_scores, axis=0).reshape(HEADS, count, WIN * WIN, count, WIN * WIN)
    eye_f = window_eye().astype(jnp.float32)
    table_terms = jnp.einsum(
        "hwivj,wv->ijh", summed, eye_f, precision=lax.Precision.HIGHEST
    ).reshape(WIN**4, HEADS)
    grad_table = lax.dot_general(
        onehot, table_terms, (((0,), (0,)), ((), ())), precision=lax.Precision.HIGHEST
    )
    total_rows = first_b.shape[0]
    grad_queries = (
        jnp.einsum("shij,sjhd->sihd", grad_scores_b, key_blocks, preferred_element_type=jnp.float32)
        * factor
    ).reshape(total_rows, DIM)
    grad_keys = jnp.einsum(
        "shij,sihd->sjhd", grad_scores_b, query_blocks, preferred_element_type=jnp.float32
    ).reshape(total_rows, DIM)
    grad_values = jnp.einsum(
        "shij,sihd->sjhd", probs_b, grad_attended, preferred_element_type=jnp.float32
    ).reshape(total_rows, DIM)
    grad_mixed_b = jnp.concatenate([grad_queries, grad_keys, grad_values], axis=1).astype(
        jnp.bfloat16
    )
    grad_qkv = inner_rows(first_b, grad_mixed_b)
    grad_first = outer_cols(grad_mixed_b, qkv_w)
    grad_gain_a = jnp.sum(grad_first * normed_a, axis=0)
    grad_shift_a = jnp.sum(grad_first, axis=0)
    grad_rows = grad_middle + norm_backward(grad_first, normed_a, scaled_a, gains_f[0])
    grad_gains = jnp.stack([grad_gain_a, grad_gain_b])
    grad_biases = jnp.stack(
        [
            grad_shift_a,
            jnp.sum(grad_queries, axis=0),
            jnp.sum(grad_values, axis=0),
            grad_proj_bias,
            grad_shift_b,
            grad_fc2_bias,
        ]
    )
    return (
        grad_rows,
        (
            grad_qkv,
            grad_proj,
            grad_fc1,
            grad_fc2,
            grad_gains,
            grad_biases,
            grad_fc1_bias,
            grad_table,
        ),
    )


def keep_slot(store, fresh, place, valid):
    former = lax.dynamic_index_in_dim(store, place, 0, keepdims=False)
    return lax.dynamic_update_index_in_dim(store, jnp.where(valid, fresh, former), place, 0)


def add_trees(left, right):
    if left is None:
        return right
    return jax.tree.map(lambda first, second: first + second, left, right)


def shards(
    images,
    cotangent,
    counts,
    regions,
    relpos,
    qkv_weight,
    proj_weight,
    fc1_weight,
    fc2_weight,
    gains,
    biases,
    fc1_bias,
    rel_table,
):
    section = lax.axis_index("section")
    later = section == 1
    offset = SHIFT * section
    micro = images.shape[0]
    slots = images.shape[1]
    live = lax.broadcasted_iota(jnp.int32, (micro, slots), 1) < counts
    onehot = relation_onehot(relpos)
    masking = region_mask(regions, later)
    zero_half = jnp.zeros((), jnp.bfloat16)
    held = (
        lax.all_gather(qkv_weight[0], "fsdp", axis=0, tiled=True),
        lax.all_gather(proj_weight[0], "fsdp", axis=0, tiled=True),
        lax.all_gather(fc1_weight[0], "fsdp", axis=0, tiled=True),
        lax.all_gather(fc2_weight[0], "fsdp", axis=0, tiled=True),
        lax.all_gather(gains[0], "fsdp", axis=1, tiled=True),
        lax.all_gather(biases[0], "fsdp", axis=1, tiled=True),
        lax.all_gather(fc1_bias[0], "fsdp", axis=0, tiled=True),
        lax.all_gather(rel_table[0], "fsdp", axis=1, tiled=True),
    )

    def fetch():
        return held

    carried = jnp.zeros(images.shape[1:], jnp.bfloat16)
    inputs_kept = jnp.zeros_like(images)
    outputs = jnp.zeros_like(images)
    for moment in range(micro + 1):
        position = moment - section
        valid = (position >= 0) & (position < micro)
        place = jnp.clip(position, 0, micro - 1)
        source = jnp.where(later, carried, images[min(moment, micro - 1)])
        params = fetch()
        added = attention_add(params[7], onehot, masking)
        result_rows, unused = forward(to_windows(source, offset), params, added)
        alive = lax.dynamic_index_in_dim(live, place, 0, keepdims=False)[:, None, None, None]
        result = jnp.where(alive, from_windows(result_rows, offset), zero_half)
        inputs_kept = keep_slot(inputs_kept, source, place, valid)
        outputs = keep_slot(outputs, result, place, valid)
        if moment < micro:
            carried = shifted(result, "section", 1)
    returned = jnp.zeros(images.shape[1:], jnp.bfloat16)
    input_grads = jnp.zeros(images.shape, jnp.float32)
    totals = None
    for moment in range(micro + 1):
        position = moment - 1 + section
        valid = (position >= 0) & (position < micro)
        place = jnp.clip(position, 0, micro - 1)
        alive = lax.dynamic_index_in_dim(live, place, 0, keepdims=False)[:, None, None, None]
        incoming = jnp.where(later, cotangent[min(moment, micro - 1)], returned)
        incoming = jnp.where(valid & alive, incoming, zero_half)
        source = lax.dynamic_index_in_dim(inputs_kept, place, 0, keepdims=False)
        params = fetch()
        added = attention_add(params[7], onehot, masking)
        unused, saved = forward(to_windows(source, offset), params, added)
        grad_rows, terms = backward(to_windows(incoming, offset), saved, params, onehot)
        grad_input = from_windows(grad_rows, offset)
        input_grads = keep_slot(input_grads, grad_input, place, valid)
        totals = add_trees(totals, terms)
        if moment < micro:
            returned = shifted(grad_input.astype(jnp.bfloat16), "section", -1)
    parted = (
        lax.psum_scatter(
            totals[0].astype(jnp.bfloat16), "fsdp", scatter_dimension=0, tiled=True
        ).astype(jnp.float32),
        lax.psum_scatter(
            totals[1].astype(jnp.bfloat16), "fsdp", scatter_dimension=0, tiled=True
        ).astype(jnp.float32),
        lax.psum_scatter(
            totals[2].astype(jnp.bfloat16), "fsdp", scatter_dimension=0, tiled=True
        ).astype(jnp.float32),
        lax.psum_scatter(
            totals[3].astype(jnp.bfloat16), "fsdp", scatter_dimension=0, tiled=True
        ).astype(jnp.float32),
        lax.psum_scatter(
            totals[4].astype(jnp.bfloat16), "fsdp", scatter_dimension=1, tiled=True
        ).astype(jnp.float32),
        lax.psum_scatter(
            totals[5].astype(jnp.bfloat16), "fsdp", scatter_dimension=1, tiled=True
        ).astype(jnp.float32),
        lax.psum_scatter(
            totals[6].astype(jnp.bfloat16), "fsdp", scatter_dimension=0, tiled=True
        ).astype(jnp.float32),
        lax.psum_scatter(
            totals[7].astype(jnp.bfloat16), "fsdp", scatter_dimension=1, tiled=True
        ).astype(jnp.float32),
    )
    shares = (
        lax.psum(parted[0].astype(jnp.bfloat16), "replica").astype(jnp.float32),
        lax.psum(parted[1].astype(jnp.bfloat16), "replica").astype(jnp.float32),
        lax.psum(parted[2].astype(jnp.bfloat16), "replica").astype(jnp.float32),
        lax.psum(parted[3].astype(jnp.bfloat16), "replica").astype(jnp.float32),
        lax.psum(parted[4].astype(jnp.bfloat16), "replica").astype(jnp.float32),
        lax.psum(parted[5].astype(jnp.bfloat16), "replica").astype(jnp.float32),
        lax.psum(parted[6].astype(jnp.bfloat16), "replica").astype(jnp.float32),
        lax.psum(parted[7].astype(jnp.bfloat16), "replica").astype(jnp.float32),
    )
    return (
        outputs[None],
        input_grads[None],
        shares[0][None],
        shares[1][None],
        shares[2][None],
        shares[3][None],
        shares[4][None],
        shares[5][None],
        shares[6][None],
        shares[7][None],
    )


def solution(mesh):
    in_specs = (
        P(None, ("fsdp", "replica"), None, None, None),
        P(None, ("fsdp", "replica"), None, None, None),
        P(None, ("fsdp", "replica")),
        P(),
        P(),
        P("section", "fsdp", None),
        P("section", "fsdp", None),
        P("section", "fsdp", None),
        P("section", "fsdp", None),
        P("section", None, "fsdp"),
        P("section", None, "fsdp"),
        P("section", "fsdp"),
        P("section", None, "fsdp"),
    )
    out_specs = (
        P("section", None, ("fsdp", "replica"), None, None, None),
        P("section", None, ("fsdp", "replica"), None, None, None),
        P("section", "fsdp", None),
        P("section", "fsdp", None),
        P("section", "fsdp", None),
        P("section", "fsdp", None),
        P("section", None, "fsdp"),
        P("section", None, "fsdp"),
        P("section", "fsdp"),
        P("section", None, "fsdp"),
    )
    return jax.shard_map(shards, mesh=mesh, in_specs=in_specs, out_specs=out_specs, check_vma=False)
```

profile of v0, /device:TPU:0, one launch (start us, length us, event | category | flops | bytes accessed | tf_op | source)
XLA Modules:
  0.0 1292.6 jit_solution(11657054412358554816)
XLA Ops:
  9.5 6.3 all-gather.1
  23.6 5.7 all-gather.3
  30.3 4.6 broadcast_in_dim.618
  34.8 5.6 broadcast_in_dim.619
  40.9 5.1 all-gather
  48.0 10.8 all-gather.4
  67.9 5.6 all-gather.6
  104.7 5.5 fusion.232
  116.6 11.8 fusion.474
  128.4 4.1 collective-permute-start
  135.8 5.3 collective-permute-done
  178.5 5.9 fusion.235
  192.4 5.1 collective-permute-start.1
  200.8 4.4 collective-permute-done.1
  242.7 5.7 fusion.238
  256.4 5.1 collective-permute-start.2
  305.9 5.9 fusion.241
  319.6 4.4 collective-permute-start.3
  375.5 4.0 fusion.449
  500.2 5.1 fusion.364
  520.8 16.6 %fusion.14 = (f32[2,16,196]{2,1,0:T(8,128)S(1)}, f32[2,16,196]{2,1,0:T(8,128)}, f32[2,16,196]{2,1,0:T(8,128)S(1)}, f32[2,16,196]{2,1,0:T(8,128)S(1)}, f32[2,16,1...) fusion(f32[16,196,196]{1,2,0:T(8,128)S(1)} %copy.870, ...), kind=kOutput, calls=%fused_computation.39 | convolution fusion | flops 100765952 | bytes 32953872 | tf_op jit(solution)/shard_map/sihd,sjhd->shij/dot_general | solution.py:137
  537.4 19.7 %fusion.13 = (f32[2,16,196,196]{2,3,1,0:T(8,128)}, f32[2,16,196,196]{2,3,1,0:T(8,128)S(1)}, f32[2,16,196,196]{2,3,1,0:T(8,128)}, f32[2,16,196,196]{2,3,1,0:T(8,128)}, f32[2,16,196,196]{2,3,1,0:T(8,128)}) fusion(f32[2,16,196,196]{2,3,1,0:T(8,128)} %get-tuple-element.238, f32[2,16,196]{2,1,0:T(8,128)S(1)} %get-tuple-element.42, f32[16,196,196]{1,2,0:T(8,128)S(1)} %copy.870, ...), kind=kLoop, calls=%fused_computation.38 | loop fusion | flops 18439680 | bytes 51794960 | tf_op jit(solution)/shard_map/div | solution.py:141
  584.3 7.0 multiply_reduce_fusion.4
  591.2 8.1 fusion.41
  603.4 5.5 fusion.636
  633.7 4.7 fusion.620
  706.9 4.8 fusion.251
  722.5 4.4 convolution_add_fusion.4
  734.2 4.2 fusion.660
  745.0 7.0 multiply_reduce_fusion.3
  752.0 7.6 fusion.43
  790.6 5.5 collective-permute-done.5
  800.7 5.2 fusion.658
  812.5 7.0 multiply_reduce_fusion.2
  819.5 7.6 fusion.45
  858.3 4.1 collective-permute-done.6
  867.0 5.2 fusion.657
  878.2 7.0 multiply_reduce_fusion.1
  885.2 7.6 fusion.47
  923.9 4.0 collective-permute-done.7
  932.5 4.4 fusion.656
  943.1 7.0 multiply_reduce_fusion
  950.1 7.7 fusion.49
  972.4 4.0 fusion.642
  980.5 4.4 fusion.40
  997.1 5.7 fusion.244
  1007.1 5.0 reshape.1263
  1012.1 12.7 copy.1077
  1024.9 8.1 fusion.661
  1044.1 6.5 reshape.1264
  1050.5 13.1 %copy.1079 = f32[16,4,49,4,49]{4,3,1,2,0:T(4,128)} copy(f32[16,4,49,4,49]{2,1,4,3,0:T(4,128)} %reshape.1264) | data formatting | bytes 4917248 | tf_op jit(solution)/shard_map/reshape | solution.py:217
  1075.0 8.0 fusion.662
  1091.2 6.7 reshape.1265
  1097.9 12.7 copy.1081
  1110.7 8.0 fusion.663
  1129.1 6.5 reshape.1266
  1135.6 12.9 copy.1083
  1148.6 8.1 fusion.664
  1172.9 4.9 reshape.1267
  1177.8 12.7 copy.1085
  1190.6 8.2 fusion.665
  1200.9 10.1 all-reduce.4
  1216.7 12.9 all-reduce.2
  1231.9 46.6 %all-reduce.7.cloned.1.call-done = (bf16[1,128,1536]{2,1,0:T(8,128)(2,1)}, bf16[1,128,512]{2,1,0:T(8,128)(2,1)}, bf16[1,128,2048]{2,1,0:T(8,128)(2,1)}, bf16[1,512,512]{2,1,0:T(8,128)(2,1)}) async-done(((bf16[1,128,1536]{2,1,0:T(8,128)(2,1)}, bf16[1,128,512]{2,1,0:T(8,128)(2,1)}, bf16[1,128,2048]{2,1,0:T(8,128)(2,1)}, bf16[1,512,512]{2,1,0:T(8,128)(2,1)}), (bf16[1,128,1536]{2,1,0:T(8,128)(2,1)}, ...) | async-done | bytes 1572880 | tf_op jit(solution)/shard_map/psum | solution.py:383
  (1149 shorter events, 777.5 us)
Async XLA Ops:
  7.2 16.0 %copy-start.195 = (s32[14,14]{1,0:T(8,128)S(1)}, s32[14,14]{1,0:T(8,128)}, u32[]{:S(2)}) copy-start(s32[14,14]{1,0:T(8,128)} %param.20) | copy-start | bytes 2356
  7.2 16.2 %copy-start.186 = (s32[49,49]{1,0:T(8,128)S(1)}, s32[49,49]{1,0:T(8,128)}, u32[]{:S(2)}) copy-start(s32[49,49]{1,0:T(8,128)} %param.21) | copy-start | bytes 28816
  7.2 16.3 %copy-start.219 = (bf16[1,169,4]{1,2,0:T(4,128)(2,1)S(1)}, bf16[1,169,4]{1,2,0:T(4,128)(2,1)}, u32[]{:S(2)}) copy-start(bf16[1,169,4]{1,2,0:T(4,128)(2,1)} %param.29) | copy-start | bytes 4060
  7.2 66.3 %all-gather.12.cloned.1.call-start = ((), (), s32[]{:S(2)}) async-start(), calls=%async_computation.10 | async-start | bytes 1966080 | tf_op jit(solution)/shard_map/all_gather | solution.py:306
  7.9 96.7 %all-gather.16.cloned.1.call-start = ((), (), s32[]{:S(2)}) async-start(), calls=%async_computation.12 | async-start | bytes 2621440 | tf_op jit(solution)/shard_map/all_gather | solution.py:309
  8.7 96.0 %all-gather.14.cloned.1.call-start = ((), (), s32[]{:S(2)}) async-start(), calls=%async_computation.11 | async-start | bytes 2621440 | tf_op jit(solution)/shard_map/all_gather | solution.py:308
  9.4 1155.6 %reduce-scatter.13.cloned.1.call-start = ((), (), s32[]{:S(2)}) async-start(), calls=%async_computation.7 | async-start | bytes 655360 | tf_op jit(solution)/shard_map/reduce_scatter | solution.py:360
  15.9 265.0 %copy-start.180 = (f32[1,1,512]{2,1,0:T(1,128)}, f32[1,1,512]{2,1,0:T(1,128)S(1)}, u32[]{:S(2)}) copy-start(f32[1,1,512]{2,1,0:T(1,128)S(1)} %get-tuple-element.197) | copy-start | bytes 6148
  15.9 265.0 %copy-start.182 = (f32[1,1,512]{2,1,0:T(1,128)}, f32[1,1,512]{2,1,0:T(1,128)S(1)}, u32[]{:S(2)}) copy-start(f32[1,1,512]{2,1,0:T(1,128)S(1)} %get-tuple-element.198) | copy-start | bytes 6148
  15.9 289.9 %copy-start.191 = (f32[1,1,512]{2,1,0:T(1,128)}, f32[1,1,512]{2,1,0:T(1,128)S(1)}, u32[]{:S(2)}) copy-start(f32[1,1,512]{2,1,0:T(1,128)S(1)} %get-tuple-element.194) | copy-start | bytes 6148
  15.9 289.9 %copy-start.221 = (f32[1,1,512]{2,1,0:T(1,128)}, f32[1,1,512]{2,1,0:T(1,128)S(1)}, u32[]{:S(2)}) copy-start(f32[1,1,512]{2,1,0:T(1,128)S(1)} %get-tuple-element.195) | copy-start | bytes 6148
  15.9 689.0 %copy-start.158 = (f32[1,1,512]{2,1,0:T(1,128)}, f32[1,1,512]{2,1,0:T(1,128)S(1)}, u32[]{:S(2)}) copy-start(f32[1,1,512]{2,1,0:T(1,128)S(1)} %get-tuple-element.196) | copy-start | bytes 6148
  23.6 11.3 copy-start.189
  40.4 18.4 %copy-start.240 = (s32[4,1]{0,1:T(1,128)S(1)}, s32[4,1]{0,1:T(1,128)}, u32[]{:S(2)}) copy-start(s32[4,1]{0,1:T(1,128)} %param.19) | copy-start | bytes 52
  46.0 259.8 %copy-start.177 = (f32[1,1,512]{2,1,0:T(1,128)}, f32[1,1,512]{2,1,0:T(1,128)S(1)}, u32[]{:S(2)}) copy-start(f32[1,1,512]{2,1,0:T(1,128)S(1)} %get-tuple-element.210) | copy-start | bytes 6148
  73.5 232.3 %copy-start.193 = (f32[1,2048]{1,0:T(1,128)}, f32[1,2048]{1,0:T(1,128)S(1)}, u32[]{:S(2)}) copy-start(f32[1,2048]{1,0:T(1,128)S(1)} %convert_element_type.889) | copy-start | bytes 24580
  128.4 12.7 collective-permute-start
  192.4 12.9 collective-permute-start.1
  248.4 13.8 %copy-start.241 = (u32[32]{0:T(128)S(1)}, u32[32]{0:T(128)}, u32[]{:S(2)}) copy-start(u32[32]{0:T(128)} %constant.267) | copy-start | bytes 388
  256.4 12.0 collective-permute-start.2
  319.6 12.5 collective-permute-start.3
  351.4 89.9 %copy-start.173 = (f32[392]{0:T(512)}, f32[392]{0:T(512)S(1)}, u32[]{:S(2)}) copy-start(f32[392]{0:T(512)S(1)} %div.360) | copy-start | bytes 4708
  355.7 83.8 %copy-start.161 = (f32[392]{0:T(512)}, f32[392]{0:T(512)S(1)}, u32[]{:S(2)}) copy-start(f32[392]{0:T(512)S(1)} %div.349) | copy-start | bytes 4708
  367.0 70.8 %copy-start.165 = (f32[392]{0:T(512)}, f32[392]{0:T(512)S(1)}, u32[]{:S(2)}) copy-start(f32[392]{0:T(512)S(1)} %div.338) | copy-start | bytes 4708
  373.5 62.6 %copy-start.169 = (f32[392]{0:T(512)}, f32[392]{0:T(512)S(1)}, u32[]{:S(2)}) copy-start(f32[392]{0:T(512)S(1)} %div.327) | copy-start | bytes 4708
  407.9 31.6 %copy-start.163 = (f32[392]{0:T(512)}, f32[392]{0:T(512)S(1)}, u32[]{:S(2)}) copy-start(f32[392]{0:T(512)S(1)} %rsqrt.215) | copy-start | bytes 4708
  410.1 10.5 copy-start.156
  416.1 21.7 %copy-start.167 = (f32[392]{0:T(512)}, f32[392]{0:T(512)S(1)}, u32[]{:S(2)}) copy-start(f32[392]{0:T(512)S(1)} %rsqrt.212) | copy-start | bytes 4708
  424.4 11.7 copy-start.171
  537.4 19.7 %copy-start.80 = (bf16[2,196,16,32]{1,0,3,2:T(2,128)(2,1)S(1)}, bf16[2,196,16,32]{1,0,3,2:T(2,128)(2,1)}, u32[]{:S(2)}) copy-start(bf16[2,196,16,32]{1,0,3,2:T(2,128)(2,1)} %reshape.1132) | copy-start | bytes 1204228
  565.3 11.8 copy-start.187
  566.4 10.7 copy-start.203
  662.8 64.1 %collective-permute-start.4 = (bf16[2,14,14,512]{3,0,2,1:T(2,128)(2,1)}, bf16[2,14,14,512]{3,0,2,1:T(2,128)(2,1)}, u32[]{:S(2)}, u32[]{:S(2)}) collective-permute-start(bf16[2,14,14,512]{3,0,2,1:T(2,128)(2,1)} %get-tuple-element.114), channel_id=1, source_target_pairs={{16,0},{17,1},{18,2},{19,3},{20,4},{21,5},{22,6},{23,7},{24,8},{25... | collective-permute-start | bytes 1204232 | tf_op jit(solution)/shard_map/ppermute | solution.py:23
  784.9 11.2 collective-permute-start.5
  852.6 9.7 collective-permute-start.6
  918.2 9.7 collective-permute-start.7
  960.7 9.1 copy-start.81
  972.3 192.7 %reduce-scatter.11.cloned.1.call-start = ((), (), s32[]{:S(2)}) async-start(), calls=%async_computation.6 | async-start | bytes 1966080 | tf_op jit(solution)/shard_map/reduce_scatter | solution.py:357
  984.9 180.1 %reduce-scatter.15.cloned.1.call-start = ((), (), s32[]{:S(2)}) async-start(), calls=%async_computation.8 | async-start | bytes 2621440 | tf_op jit(solution)/shard_map/reduce_scatter | solution.py:363
  997.0 9.9 copy-start.184
  997.0 10.0 copy-start.185
  997.0 168.1 %reduce-scatter.17.cloned.1.call-start = ((), (), s32[]{:S(2)}) async-start(), calls=%async_computation.9 | async-start | bytes 2621440 | tf_op jit(solution)/shard_map/reduce_scatter | solution.py:366
  997.1 10.0 copy-start.28
  1012.1 12.7 copy-start.179
  1024.8 9.4 copy-start.200
  1024.8 9.4 copy-start.210
  1024.8 9.4 copy-start.211
  1024.8 9.4 copy-start.150
  1074.9 11.5 copy-start.201
  1074.9 11.5 copy-start.212
  1075.0 11.5 copy-start.213
  1075.0 140.1 %reduce-scatter.19.cloned.1.call-start = ((), (), s32[]{:S(2)}) async-start(), calls=%async_computation.13 | async-start | bytes 163840
  1110.7 11.4 copy-start.202
  1110.7 11.4 copy-start.214
  1110.7 11.4 copy-start.215
  1148.5 10.5 copy-start.6
  1148.6 10.5 copy-start.26
  1164.0 51.9 %reduce-scatter.21.cloned.1.call-start = ((), (), s32[]{:S(2)}) async-start(), calls=%async_computation.14 | async-start | bytes 163840
  1164.9 113.6 %all-reduce.7.cloned.1.call-start = ((), (), s32[]{:S(2)}) async-start(), calls=%async_computation.15 | async-start | bytes 3145728 | tf_op jit(solution)/shard_map/psum | solution.py:383
  1190.5 9.4 copy-start.160
  1190.5 9.4 copy-start.250
  1190.6 9.4 copy-start.251
  1190.6 9.4 copy-start.252
  1190.6 20.5 %copy-start.125 = (f32[2,2,7,2,7,512]{5,0,4,3,2,1:T(2,128)S(1)}, f32[2,2,7,2,7,512]{5,0,4,3,2,1:T(2,128)}, u32[]{:S(2)}) copy-start(f32[2,2,7,2,7,512]{5,0,4,3,2,1:T(2,128)} %copy.1044) | copy-start | bytes 2408452
  (216 other events, 897.7 us)
Sparse Core Ops, SparseCore 0:
  9.6 22.4 all-gather.11
  33.6 23.9 all-gather.15
  59.2 22.3 all-gather.13
  972.4 20.7 reduce-scatter.12
  995.6 28.0 reduce-scatter.10
  1026.1 31.1 reduce-scatter.14
  1075.1 31.0 reduce-scatter.16
  1164.1 19.4 reduce-scatter.18
  1186.6 19.7 reduce-scatter.20
  1208.8 69.6 all-reduce.6
where the time goes:
time: 1310 us; the launch traced here: 1290 us
  local copies, waits for them, and re-layouts  503 us (38%)
  matrix products  377 us (29%)
  other arithmetic  239 us (18%)
  waiting for transfers between devices  73.6 us (6%)
  blocking collectives  56.6 us (4%)
  starting transfers between devices  24.5 us (2%)
  between operations  19.3 us (1%)
    reshape x10, local copies, waits for them, and re-layouts, backward(): jnp.sum(grad_scores, axis=0)  93.8 us
    dot_general x10, matrix products, forward(): jnp.einsum('sihd,sjhd->shij', query_blocks, key_blocks, preferred_element...  49.7 us
    dot_general x20, matrix products, outer_cols(): lax.dot_general(left, right, (((1,), (1,)), ((), ())), preferred_element_...  49.6 us
    dot_general x20, matrix products, inner_rows(): lax.dot_general(left, right, (((0,), (0,)), ((), ())), preferred_element_...  47 us
    psum x1, waiting for transfers between devices, shards(): lax.psum(parted[0].astype(jnp.bfloat16), 'replica').astype(jnp.float32)  46.6 us
    dynamic_update_slice x15, other arithmetic, keep_slot(): lax.dynamic_update_index_in_dim(store, jnp.where(valid, fresh, former), p...  46.5 us
    unnamed x544, local copies, waits for them, and re-layouts  46.2 us
    dot_general x5, matrix products, backward(): jnp.einsum('hwivj,wv->ijh', summed, eye_f, precision=lax.Precision.HIGHEST)  40.3 us
  transfers between devices with their start and end apart: 18, of which 7 were waited for; matrix products, arithmetic and copies ran while one was open for 29% of the time, Pallas kernels for 0%

commit v1 on v0

v1 whole, which is shorter than its diff:
```python
import jax
import jax.numpy as jnp
from jax import lax
from jax.experimental import pallas as pl
from jax.experimental.pallas import tpu as pltpu
from jax.sharding import PartitionSpec as P

DIM = 512
HEADS = 16
HEAD_DIM = 32
HIDDEN = 2048
WIN = 7
SIDE = 14
SHIFT = 3
TABLE = 169

AREA = WIN * WIN
PARTS = (SIDE // WIN) ** 2
SPAN = 64
ROWS = PARTS * SPAN
LINE = 16
FLAT = SIDE * LINE
GROUP = 8
GROUPS = HEADS // GROUP
KEYS = GROUP * SPAN
FEAT = GROUP * HEAD_DIM
CHUNK = 512
CHUNKS = HIDDEN // CHUNK
SUMS = 16

EPSILON = 1e-05
ROOT_HALF = 0.7071067811865476
INV_ROOT_TAU = 0.3989422804014327
FACTOR = HEAD_DIM ** (-0.5)
NEVER = -1e30

BF = jnp.bfloat16
F32 = jnp.float32


def nn(left, right):
    return lax.dot_general(left, right, (((1,), (0,)), ((), ())), preferred_element_type=F32)


def nt(left, right):
    return lax.dot_general(left, right, (((1,), (1,)), ((), ())), preferred_element_type=F32)


def tn(left, right):
    return lax.dot_general(left, right, (((0,), (0,)), ((), ())), preferred_element_type=F32)


def normalize(values):
    center = values - jnp.mean(values, axis=-1, keepdims=True)
    spread = jnp.mean(center * center, axis=-1, keepdims=True)
    scaled = lax.rsqrt(spread + EPSILON)
    return center * scaled, scaled


def norm_backward(direct, normed, scaled):
    return (
        direct
        - jnp.mean(direct, axis=-1, keepdims=True)
        - normed * jnp.mean(direct * normed, axis=-1, keepdims=True)
    ) * scaled


def fold_heads(stacked, own):
    kept = stacked * own
    total = kept[:SPAN]
    for head in range(1, GROUP):
        total = total + kept[head * SPAN : (head + 1) * SPAN]
    return total


def spread_heads(rows, own):
    return jnp.concatenate([rows] * GROUP, axis=0) * own


def load_image(first_ref, second_ref, later, flat_ref):
    @pl.when(later == 0)
    def _():
        for row in range(SIDE):
            flat_ref[row * LINE : row * LINE + SIDE, :] = first_ref[0, 0, row]

    @pl.when(later != 0)
    def _():
        for row in range(SIDE):
            flat_ref[row * LINE : row * LINE + SIDE, :] = second_ref[0, 0, row]


def forward_kernel(
    info,
    images_ref,
    carried_ref,
    perm_ref,
    back_ref,
    added_ref,
    own_ref,
    same_ref,
    qkv_ref,
    proj_ref,
    fc1_ref,
    fc2_ref,
    rows_ref,
    hidden_ref,
    *rest,
):
    (out_ref, send_ref, n1_ref, h1_ref, scale_ref, mix_ref, p_ref, o_ref, n2_ref, h2_ref, u_ref, slope_ref) = rest[-13:-1]
    flat_ref = rest[-1]
    slot = pl.program_id(0)

    @pl.when(slot == 0)
    def _():
        flat_ref[...] = jnp.zeros_like(flat_ref)

    load_image(images_ref, carried_ref, info[1], flat_ref)
    base = nn(perm_ref[...], flat_ref[...])
    normed_a, scaled_a = normalize(base)
    n1_ref[0, 0] = normed_a.astype(BF)
    first = (normed_a * rows_ref[0:1, :] + rows_ref[2:3, :]).astype(BF)
    h1_ref[0, 0] = first
    scale_ref[0, 0, :, 0:128] = jnp.broadcast_to(scaled_a, (ROWS, 128))
    query = ((nn(first, qkv_ref[:, :DIM]) + rows_ref[3:4, :]) * FACTOR).astype(BF)
    mix_ref[0, 0, :, :DIM] = query
    key = nn(first, qkv_ref[:, DIM : 2 * DIM]).astype(BF)
    mix_ref[0, 0, :, DIM : 2 * DIM] = key
    value = (nn(first, qkv_ref[:, 2 * DIM :]) + rows_ref[4:5, :]).astype(BF)
    mix_ref[0, 0, :, 2 * DIM :] = value
    own = own_ref[...]
    same = same_ref[...]
    for window in range(PARTS):
        at = slice(window * SPAN, (window + 1) * SPAN)
        for group in range(GROUPS):
            feats = slice(group * FEAT, (group + 1) * FEAT)
            keys = slice(group * KEYS, (group + 1) * KEYS)
            scores = nt(query[at, feats], spread_heads(key[at, feats], own)) + added_ref[window, :, keys]
            expo = jnp.exp(scores)
            total = nn(expo.astype(BF), same)
            probs = (expo / total).astype(BF)
            p_ref[0, 0, at, keys] = probs
            o_ref[0, 0, at, feats] = nn(probs, spread_heads(value[at, feats], own)).astype(BF)
    middle = base + nn(o_ref[0, 0], proj_ref[...]) + rows_ref[5:6, :]
    normed_b, scaled_b = normalize(middle)
    n2_ref[0, 0] = normed_b.astype(BF)
    scale_ref[0, 0, :, 128:256] = jnp.broadcast_to(scaled_b, (ROWS, 128))
    second = (normed_b * rows_ref[1:2, :] + rows_ref[6:7, :]).astype(BF)
    h2_ref[0, 0] = second
    output = middle + rows_ref[7:8, :]
    for chunk in range(CHUNKS):
        cols = slice(chunk * CHUNK, (chunk + 1) * CHUNK)
        before = nn(second, fc1_ref[:, cols]) + hidden_ref[0:1, cols]
        share = 0.5 * (1.0 + lax.erf(before * ROOT_HALF))
        hidden = (before * share).astype(BF)
        u_ref[0, 0, :, cols] = hidden
        slope_ref[0, 0, :, cols] = (
            share + before * INV_ROOT_TAU * jnp.exp(-0.5 * before * before)
        ).astype(BF)
        output = output + nn(hidden, fc2_ref[cols, :])
    alive = (slot < info[2]).astype(F32)
    image = (nn(back_ref[...], output.astype(BF)) * alive).astype(BF)
    for row in range(SIDE):
        line = image[row * LINE : row * LINE + SIDE]
        out_ref[0, 0, row] = line
        send_ref[0, 0, row] = line


def backward_kernel(
    info,
    cotangent_ref,
    returned_ref,
    perm_ref,
    back_ref,
    own_ref,
    match_ref,
    qkv_ref,
    proj_ref,
    fc1_ref,
    fc2_ref,
    rows_ref,
    n1_ref,
    scale_ref,
    mix_ref,
    p_ref,
    o_ref,
    n2_ref,
    slope_ref,
    *rest,
):
    (grad_ref, send_ref, gy_ref, dab_ref, drb_ref, dmb_ref, sums_ref, table_ref) = rest[-10:-2]
    flat_ref, dob_ref = rest[-2:]
    slot = pl.program_id(0)

    @pl.when(slot == 0)
    def _():
        flat_ref[...] = jnp.zeros_like(flat_ref)

    load_image(returned_ref, cotangent_ref, info[1], flat_ref)
    alive = (slot < info[2]).astype(F32)
    upstream = nn(perm_ref[...], flat_ref[...]) * alive
    upstream_b = upstream.astype(BF)
    gy_ref[0, 0] = upstream_b
    sums_ref[0, 0, 12:16, :] = jnp.zeros((4, DIM), F32)
    sums_ref[0, 0, 7:8, :] = jnp.sum(upstream, axis=0, keepdims=True)
    grad_second = jnp.zeros((ROWS, DIM), F32)
    for chunk in range(CHUNKS):
        cols = slice(chunk * CHUNK, (chunk + 1) * CHUNK)
        grad_before = nt(upstream_b, fc2_ref[cols, :]) * slope_ref[0, 0, :, cols].astype(F32)
        sums_ref[0, 0, 8 + chunk : 9 + chunk, :] = jnp.sum(grad_before, axis=0, keepdims=True)
        grad_before_b = grad_before.astype(BF)
        dab_ref[0, 0, :, cols] = grad_before_b
        grad_second = grad_second + nt(grad_before_b, fc1_ref[:, cols])
    normed_b = n2_ref[0, 0].astype(F32)
    sums_ref[0, 0, 1:2, :] = jnp.sum(grad_second * normed_b, axis=0, keepdims=True)
    sums_ref[0, 0, 6:7, :] = jnp.sum(grad_second, axis=0, keepdims=True)
    grad_middle = upstream + norm_backward(
        grad_second * rows_ref[1:2, :], normed_b, scale_ref[0, 0, :, 128:129]
    )
    grad_middle_b = grad_middle.astype(BF)
    drb_ref[0, 0] = grad_middle_b
    sums_ref[0, 0, 5:6, :] = jnp.sum(grad_middle, axis=0, keepdims=True)
    dob_ref[...] = nt(grad_middle_b, proj_ref[...]).astype(BF)
    own = own_ref[...]
    own_f = own.astype(F32)
    match = match_ref[...]
    for window in range(PARTS):
        at = slice(window * SPAN, (window + 1) * SPAN)
        for group in range(GROUPS):
            feats = slice(group * FEAT, (group + 1) * FEAT)
            keys = slice(group * KEYS, (group + 1) * KEYS)
            query = mix_ref[0, 0, at, group * FEAT : (group + 1) * FEAT]
            key = mix_ref[0, 0, at, DIM + group * FEAT : DIM + (group + 1) * FEAT]
            value = mix_ref[0, 0, at, 2 * DIM + group * FEAT : 2 * DIM + (group + 1) * FEAT]
            probs = p_ref[0, 0, at, keys]
            grad_out = dob_ref[at, feats]
            grad_probs = nt(grad_out, spread_heads(value, own))
            level = grad_out.astype(F32) * o_ref[0, 0, at, feats].astype(F32)
            mean = nn(level.astype(BF), match)
            grad_scores = probs.astype(F32) * (grad_probs - mean)
            if window == 0:
                table_ref[0, 0, :, keys] = grad_scores
            else:
                table_ref[0, 0, :, keys] += grad_scores
            grad_scores_b = grad_scores.astype(BF)
            grad_query = nn(grad_scores_b, spread_heads(key, own)) * FACTOR
            grad_key = fold_heads(tn(grad_scores_b, query), own_f)
            grad_value = fold_heads(tn(probs, grad_out), own_f)
            dmb_ref[0, 0, at, group * FEAT : (group + 1) * FEAT] = grad_query.astype(BF)
            dmb_ref[0, 0, at, DIM + group * FEAT : DIM + (group + 1) * FEAT] = grad_key.astype(BF)
            dmb_ref[0, 0, at, 2 * DIM + group * FEAT : 2 * DIM + (group + 1) * FEAT] = grad_value.astype(BF)
            add_query = jnp.sum(grad_query, axis=0, keepdims=True)
            add_value = jnp.sum(grad_value, axis=0, keepdims=True)
            if window == 0:
                sums_ref[0, 0, 3:4, feats] = add_query
                sums_ref[0, 0, 4:5, feats] = add_value
            else:
                sums_ref[0, 0, 3:4, feats] += add_query
                sums_ref[0, 0, 4:5, feats] += add_value
    grad_first = nt(dmb_ref[0, 0], qkv_ref[...])
    normed_a = n1_ref[0, 0].astype(F32)
    sums_ref[0, 0, 0:1, :] = jnp.sum(grad_first * normed_a, axis=0, keepdims=True)
    sums_ref[0, 0, 2:3, :] = jnp.sum(grad_first, axis=0, keepdims=True)
    grad_rows = grad_middle + norm_backward(
        grad_first * rows_ref[0:1, :], normed_a, scale_ref[0, 0, :, 0:1]
    )
    image = nn(back_ref[...], grad_rows.astype(BF))
    image_b = image.astype(BF)
    for row in range(SIDE):
        grad_ref[0, 0, row] = image[row * LINE : row * LINE + SIDE]
        send_ref[0, 0, row] = image_b[row * LINE : row * LINE + SIDE]


def whole(array):
    rank = array.ndim
    return pl.BlockSpec(array.shape, lambda i, info: (0,) * rank, pipeline_mode=pl.Buffered(1))


def image_shape(lead, dtype):
    return jax.ShapeDtypeStruct(lead + (SIDE, SIDE, DIM), dtype)


def at_place(shape):
    tail = shape[2:]
    zeros = (0,) * len(tail)
    return pl.BlockSpec((1, 1) + tail, lambda i, info: (info[0], i) + zeros)


def at_slot(shape):
    tail = shape[2:]
    zeros = (0,) * len(tail)
    return pl.BlockSpec((1, 1) + tail, lambda i, info: (0, i) + zeros)


def run(kernel, info, ins, in_specs, outs, out_specs, stores, scratch, name, after=None):
    slots = outs[0].shape[1]
    aliases = {}
    args = [info] + list(ins)
    specs = list(in_specs)
    if stores is not None:
        for position, store in stores:
            aliases[len(args)] = position
            args.append(store)
            specs.append(pl.BlockSpec(memory_space=pl.ANY))
    if after is not None:
        args.append(after)
        specs.append(pl.BlockSpec(memory_space=pl.ANY))
    return pl.pallas_call(
        kernel,
        out_shape=outs,
        grid_spec=pltpu.PrefetchScalarGridSpec(
            num_scalar_prefetch=1,
            grid=(slots,),
            in_specs=specs,
            out_specs=out_specs,
            scratch_shapes=scratch,
        ),
        input_output_aliases=aliases,
        compiler_params=pltpu.CompilerParams(
            dimension_semantics=("arbitrary",), vmem_limit_bytes=58 << 20
        ),
        name=name,
    )(*args)


def token_places(offset):
    index = lax.broadcasted_iota(jnp.int32, (ROWS, FLAT), 0)
    window, inner = index // SPAN, index % SPAN
    line = (window // 2) * WIN + inner // WIN + offset
    column = (window % 2) * WIN + inner % WIN + offset
    line = jnp.where(line >= SIDE, line - SIDE, line)
    column = jnp.where(column >= SIDE, column - SIDE, column)
    return jnp.where(inner < AREA, line * LINE + column, -1)


def attention_add(table, relpos, regions, later):
    onehot = (relpos.reshape(AREA, AREA)[:, :, None] == jnp.arange(TABLE, dtype=jnp.int32)).astype(BF)
    lookup = lax.dot_general(onehot, table, (((2,), (0,)), ((), ())), preferred_element_type=F32)
    lookup = lookup.transpose(0, 2, 1)
    lookup = jnp.pad(
        lookup, ((0, SPAN - AREA), (0, 0), (0, SPAN - AREA)), constant_values=0.0
    )
    side = SIDE // WIN
    tiles = regions.reshape(side, WIN, side, WIN).transpose(0, 2, 1, 3).reshape(PARTS, AREA)
    tiles = jnp.pad(tiles, ((0, 0), (0, SPAN - AREA)))
    shape = (PARTS, SPAN, SPAN)
    present = lax.broadcasted_iota(jnp.int32, shape, 1) < AREA
    differ = (tiles[:, :, None] != tiles[:, None, :]) & later & present
    mask = jnp.where(differ, F32(-100.0), F32(0.0))
    absent = lax.broadcasted_iota(jnp.int32, shape, 2) >= AREA
    mask = jnp.where(absent, F32(NEVER), mask)
    return (lookup[None] + mask[:, :, None, :]).reshape(PARTS, SPAN, HEADS * SPAN)


def table_gradient(summed, relpos):
    pairs = summed.reshape(SPAN, HEADS, SPAN)[:AREA, :, :AREA]
    onehot = (relpos[:, :, None] == jnp.arange(TABLE, dtype=jnp.int32)).astype(F32)
    return lax.dot_general(
        onehot.reshape(AREA * AREA, TABLE),
        pairs.transpose(0, 2, 1).reshape(AREA * AREA, HEADS),
        (((0,), (0,)), ((), ())),
        precision=lax.Precision.HIGHEST,
        preferred_element_type=F32,
    )


def shifted(value, axis, by):
    length = lax.axis_size(axis)
    pairs = [(i, i + by) for i in range(length) if 0 <= i + by < length]
    return lax.ppermute(value, axis, pairs)


def shards(
    images,
    cotangent,
    counts,
    regions,
    relpos,
    qkv_weight,
    proj_weight,
    fc1_weight,
    fc2_weight,
    gains,
    biases,
    fc1_bias,
    rel_table,
):
    section = lax.axis_index("section")
    later = section == 1
    flag = later.astype(jnp.int32)
    micro, slots = images.shape[:2]
    pieces = lax.axis_size("fsdp")
    width = DIM // pieces

    small = jnp.concatenate(
        [gains[0].reshape(-1), biases[0].reshape(-1), fc1_bias[0].reshape(-1), rel_table[0].reshape(-1)]
    )
    small = jnp.pad(small, (0, -small.shape[0] % 1024)).reshape(-1, 128)
    small = lax.all_gather(small, "fsdp", axis=0, tiled=False).reshape(pieces, -1)
    qkv_w = lax.all_gather(qkv_weight[0], "fsdp", axis=0, tiled=True)
    proj_w = lax.all_gather(proj_weight[0], "fsdp", axis=0, tiled=True)
    fc1_w = lax.all_gather(fc1_weight[0], "fsdp", axis=0, tiled=True)
    fc2_w = lax.all_gather(fc2_weight[0], "fsdp", axis=0, tiled=True)
    cut_a, cut_b = 8 * width, 8 * width + HIDDEN // pieces
    rows = small[:, :cut_a].reshape(pieces, 8, width).transpose(1, 0, 2).reshape(8, DIM).astype(F32)
    hidden_bias = small[:, cut_a:cut_b].reshape(1, HIDDEN).astype(F32)
    per_piece = HEADS // pieces
    table = small[:, cut_b : cut_b + TABLE * per_piece].reshape(pieces, TABLE, per_piece)
    table = table.transpose(1, 0, 2).reshape(TABLE, HEADS)

    places = token_places(SHIFT * flag)
    perm = (places == lax.broadcasted_iota(jnp.int32, (ROWS, FLAT), 1)).astype(BF)
    back = perm.T
    added = attention_add(table, relpos, regions, later)
    key_head = lax.broadcasted_iota(jnp.int32, (KEYS, FEAT), 0) // SPAN
    own = (key_head == lax.broadcasted_iota(jnp.int32, (KEYS, FEAT), 1) // HEAD_DIM).astype(BF)
    match = own.T
    same = (
        lax.broadcasted_iota(jnp.int32, (KEYS, KEYS), 0) // SPAN
        == lax.broadcasted_iota(jnp.int32, (KEYS, KEYS), 1) // SPAN
    ).astype(BF)

    lead = (micro, slots)
    bank = lambda width, dtype=BF, rows=ROWS: jax.ShapeDtypeStruct(lead + (rows, width), dtype)
    small_lead = (1, slots)
    send_shape = image_shape(small_lead, BF)
    fwd_outs = (
        image_shape(lead, BF),
        send_shape,
        bank(DIM),
        bank(DIM),
        bank(256, F32),
        bank(3 * DIM),
        bank(HEADS * SPAN),
        bank(DIM),
        bank(DIM),
        bank(DIM),
        bank(HIDDEN),
        bank(HIDDEN),
    )
    bwd_outs = (
        image_shape(lead, F32),
        send_shape,
        bank(DIM),
        bank(HIDDEN),
        bank(DIM),
        bank(3 * DIM),
        bank(DIM, F32, SUMS),
        bank(HEADS * SPAN, F32, SPAN),
    )
    specs_of = lambda outs: tuple(
        at_slot(o.shape) if i == 1 else at_place(o.shape) for i, o in enumerate(outs)
    )
    weights = (qkv_w, proj_w, fc1_w, fc2_w)

    def describe(position):
        place = jnp.clip(position, 0, micro - 1)
        count = lax.dynamic_index_in_dim(counts[:, 0], place, 0, keepdims=False)
        return jnp.stack([place, flag, count]).astype(jnp.int32)

    def forward_step(position, carried, held, after):
        info = describe(position)
        consts = (perm, back, added, own, same) + weights + (rows, hidden_bias)
        ins = (images, carried) + consts
        in_specs = [at_place(images.shape), at_slot(carried.shape)] + [whole(c) for c in consts]
        stores = None if held is None else [(i, h) for i, h in enumerate(held) if i != 1]
        return run(
            forward_kernel, info, ins, in_specs, fwd_outs, specs_of(fwd_outs), stores,
            [pltpu.VMEM((FLAT, DIM), BF)], "forward", after,
        )

    def backward_step(position, returned, saved, held, after):
        info = describe(position)
        consts = (perm, back, own, match) + weights + (rows,)
        kept = (saved[2], saved[4], saved[5], saved[6], saved[7], saved[8], saved[11])
        ins = (cotangent, returned) + consts + kept
        in_specs = (
            [at_place(cotangent.shape), at_slot(returned.shape)]
            + [whole(c) for c in consts]
            + [at_place(k.shape) for k in kept]
        )
        stores = None if held is None else [(i, h) for i, h in enumerate(held) if i != 1]
        return run(
            backward_kernel, info, ins, in_specs, bwd_outs, specs_of(bwd_outs), stores,
            [pltpu.VMEM((FLAT, DIM), BF), pltpu.VMEM((ROWS, DIM), BF)], "backward", after,
        )

    carried = jnp.zeros(send_shape.shape, BF)
    returned = jnp.zeros(send_shape.shape, BF)
    saved = grads = None
    for moment in range(micro + 2):
        if moment <= micro:
            after = None if grads is None else grads[6]
            saved = forward_step(moment - flag, carried, saved, after)
            if moment < micro:
                carried = shifted(saved[1], "section", 1)
        if moment >= 1:
            grads = backward_step(moment - 2 + flag, returned, saved, grads, None)
            if moment <= micro:
                returned = shifted(grads[1], "section", -1)

    flat = lambda a: a.reshape(-1, a.shape[-1])
    h1, o, h2, u = (flat(saved[i]) for i in (3, 7, 9, 10))
    gy, dab, drb, dmb = (flat(grads[i]) for i in (2, 3, 4, 5))
    big = [tn(u, gy), tn(h2, dab), tn(h1, dmb), tn(o, drb)]
    big = [lax.psum_scatter(b.astype(BF), "fsdp", scatter_dimension=0, tiled=True) for b in big]
    big = [lax.psum(b, "replica").astype(F32)[None] for b in big]
    sums = jnp.sum(grads[6], axis=(0, 1))
    table_grad = table_gradient(jnp.sum(grads[7], axis=(0, 1)), relpos)
    spread = jnp.concatenate(
        [
            sums[:8].reshape(8, pieces, width).transpose(1, 0, 2).reshape(pieces, -1),
            sums[8:12].reshape(pieces, -1),
            table_grad.reshape(TABLE, pieces, per_piece).transpose(1, 0, 2).reshape(pieces, -1),
        ],
        axis=1,
    )
    spread = jnp.pad(spread, ((0, 0), (0, -spread.shape[1] % 1024)))
    total = lax.psum(lax.psum_scatter(spread, "fsdp", scatter_dimension=0, tiled=True), "replica")[0]
    vectors = total[:cut_a].reshape(8, width)
    return (
        saved[0][None],
        grads[0][None],
        big[2],
        big[3],
        big[1],
        big[0],
        vectors[None, :2],
        vectors[None, 2:],
        total[None, cut_a:cut_b],
        total[cut_b : cut_b + TABLE * per_piece].reshape(1, TABLE, per_piece),
    )


def solution(mesh):
    in_specs = (
        P(None, ("fsdp", "replica"), None, None, None),
        P(None, ("fsdp", "replica"), None, None, None),
        P(None, ("fsdp", "replica")),
        P(),
        P(),
        P("section", "fsdp", None),
        P("section", "fsdp", None),
        P("section", "fsdp", None),
        P("section", "fsdp", None),
        P("section", None, "fsdp"),
        P("section", None, "fsdp"),
        P("section", "fsdp"),
        P("section", None, "fsdp"),
    )
    out_specs = (
        P("section", None, ("fsdp", "replica"), None, None, None),
        P("section", None, ("fsdp", "replica"), None, None, None),
        P("section", "fsdp", None),
        P("section", "fsdp", None),
        P("section", "fsdp", None),
        P("section", "fsdp", None),
        P("section", None, "fsdp"),
        P("section", None, "fsdp"),
        P("section", "fsdp"),
        P("section", None, "fsdp"),
    )
    return jax.shard_map(shards, mesh=mesh, in_specs=in_specs, out_specs=out_specs, check_vma=False)
```

time: 1310 us -> 552 us (0.42)
  local copies, waits for them, and re-layouts: 503 us -> 32.6 us
  matrix products: 377 us -> 32.4 us
  other arithmetic: 239 us -> 24.8 us
  Pallas kernels: 0 us -> 194 us
  waiting for transfers between devices: 73.6 us -> 174 us
    dot_general x121 -> x6, matrix products: 377 us -> 32.4 us  [the longest x4 30.6 us: tn(): lax.dot_general(left, right, (((0,), (0,)), ((), ())), preferred_element_...]
    reshape x93 -> x9, local copies, waits for them, and re-layouts: 233 us -> 1.7 us  [the longest x3 0.86 us: attention_add(): regions.reshape(side, WIN, side, WIN).transpose(0, 2, 1, 3)]
    pallas_call x0 -> x10, Pallas kernels: none -> 194 us  [run(): pl.pallas_call(kernel, out_shape=outs, grid_spec=pltpu.PrefetchScalarGrid...]
    convert_element_type x55 -> x0, local copies, waits for them, and re-layouts: 95.2 us -> none  [the longest x20 36.2 us: forward(): base = rows.astype(jnp.float32)]
    reduce_scatter x4, waiting for transfers between devices: 0.08 us -> 84.4 us  [shards(): lax.psum_scatter(b.astype(BF), 'fsdp', scatter_dimension=0, tiled=True)]
    reduce_sum x45 -> x2, other arithmetic: 70.3 us -> 0.16 us  [the longest x1 0.14 us: shards(): table_grad = table_gradient(jnp.sum(grads[7], axis=(0, 1)), relpos)]
    concatenate x37 -> x1, other arithmetic: 48.8 us -> 0.01 us  [shards(): jnp.concatenate([sums[:8].reshape(8, pieces, width).transpose(1, 0, 2).re...]
    dynamic_update_slice x15 -> x0, other arithmetic: 46.5 us -> none  [keep_slot(): lax.dynamic_update_index_in_dim(store, jnp.where(valid, fresh, former), p...]
  transfers between devices with their start and end apart: 18 -> 16, of which waited for: 7 -> 8; matrix products, arithmetic and copies ran while one was open for 29% -> 13% of each run, Pallas kernels for 0% -> 21%
where the time goes in v1:
time: 552 us; the launch traced here: 544 us
  Pallas kernels  194 us (35%)
  waiting for transfers between devices  174 us (32%)
  blocking collectives  47.6 us (9%)
  local copies, waits for them, and re-layouts  32.6 us (6%)
  matrix products  32.4 us (6%)
  other arithmetic  24.8 us (4%)
  starting transfers between devices  23.8 us (4%)
  between operations  15.2 us (3%)
    pallas_call x10, Pallas kernels, run(): pl.pallas_call(kernel, out_shape=outs, grid_spec=pltpu.PrefetchScalarGrid...  194 us
    reduce_scatter x4, waiting for transfers between devices, shards(): lax.psum_scatter(b.astype(BF), 'fsdp', scatter_dimension=0, tiled=True)  84.4 us
    dot_general x4, matrix products, tn(): lax.dot_general(left, right, (((0,), (0,)), ((), ())), preferred_element_...  30.6 us
    psum x1, waiting for transfers between devices, shards(): big = [lax.psum(b, 'replica').astype(F32)[None] for b in big]  29.5 us
    unnamed x64, local copies, waits for them, and re-layouts  26.5 us
    all_gather x1, waiting for transfers between devices, shards(): fc2_w = lax.all_gather(fc2_weight[0], 'fsdp', axis=0, tiled=True)  24.2 us
    ppermute x8, starting transfers between devices, shifted(): return lax.ppermute(value, axis, pairs)  23.3 us
    psum x1, blocking collectives, shards(): lax.psum(lax.psum_scatter(spread, 'fsdp', scatter_dimension=0, tiled=True...  20.4 us
  transfers between devices with their start and end apart: 16, of which 8 were waited for; matrix products, arithmetic and copies ran while one was open for 13% of the time, Pallas kernels for 21%

profile of v1, /device:TPU:0, one launch (start us, length us, event | category | flops | bytes accessed | tf_op | source)
XLA Modules:
  0.0 544.2 jit_solution(9292377371870831215)
XLA Ops:
  9.5 0.8 reshape.123
  10.5 1.6 copy.167.images_ref
  13.3 6.2 %all_gather.15 = bf16[4,24,128]{2,1,0:T(8,128)(2,1)S(1)} all-gather(bf16[1,24,128]{2,1,0:T(8,128)(2,1)S(1)} %fusion.62), channel_id=1, replica_groups=mesh['section'=2,'fsdp'=4,'replica'=4] {'fsdp'}, dimensions={0}, use_global_device_ids=true | all-gather | bytes 30720 | tf_op jit(solution)/shard_map/all_gather | solution.py:398
  20.0 0.8 fusion.7
  22.9 1.3 pad_add_fusion.4.info
  24.3 10.3 %all-gather.1 = bf16[1,512,512]{2,1,0:T(8,128)(2,1)} all-gather(bf16[1,128,512]{2,1,0:T(8,128)(2,1)S(1)} %copy-done.16), channel_id=3, replica_groups=mesh['section'=2,'fsdp'=4,'replica'=4] {'fsdp'}, dimensions={1}, use_global_device_ids=true | all-gather | bytes 655360 | tf_op jit(solution)/shard_map/all_gather | solution.py:400
  35.3 1.0 fusion.17.own_ref
  36.3 1.1 fusion.38.perm_ref
  37.4 1.1 fusion.11.same_ref
  38.4 1.1 broadcast_add_fusion.added_ref
  39.5 18.5 %all-gather.10.cloned.1.call-done = bf16[1,512,2048]{2,1,0:T(8,128)(2,1)} async-done(((bf16[1,128,2048]{2,1,0:T(8,128)(2,1)}), bf16[1,512,2048]{2,1,0:T(8,128)(2,1)}) %all-gather.10.cloned.1.call-update) | async-done | bytes 2097168 | tf_op jit(solution)/shard_map/all_gather | solution.py:401
  58.0 24.2 %all-gather.12.cloned.1.call-done = bf16[1,2048,512]{2,1,0:T(8,128)(2,1)} async-done(((bf16[1,512,512]{2,1,0:T(8,128)(2,1)}), bf16[1,2048,512]{2,1,0:T(8,128)(2,1)}) %all-gather.12.cloned.1.call-update) | async-done | bytes 2097168 | tf_op jit(solution)/shard_map/all_gather | solution.py:402
  82.2 0.8 broadcast_6_carried_ref_returned_ref.2.carried_ref.returned_ref
  83.0 20.0 %forward.5 = (bf16[4,2,14,14,512]{4,3,2,1,0:T(8,128)(2,1)}, bf16[1,2,14,14,512]{4,3,2,1,0:T(8,128)(2,1)}, bf16[4,2,256,512]{3,2,1,0:T(8,128)(2,1)}, bf16[4,2,256...) custom-call(s32[3]{0:T(128)} %pad_add_fusion.4.info, ...), custom_call_target="tpu_custom_call" | custom-call | tf_op jit(solution)/shard_map/forward/pallas_call | solution.py:307
  103.0 3.6 collective-permute-start
  106.6 1.7 copy.162.cotangent_ref
  108.3 1.9 pad_add_fusion.3
  110.3 0.9 fusion.18.match_ref
  111.2 5.7 %collective-permute-done.carried_ref = bf16[1,2,14,14,512]{4,3,2,1,0:T(8,128)(2,1)S(1)} collective-permute-done((bf16[1,2,14,14,512]{4,3,2,1,0:T(8,128)(2,1)}, bf16[1,2,14,14,512]{4,3,2,1,0:T(8,128)(2,1)S(1)}, u32[]{:S(2)}, u32[]{:S(2)}) %collective-permute-start) | collective-permute-done | bytes 401440 | tf_op jit(solution)/shard_map/ppermute | solution.py:369
  117.7 19.8 %forward.6 = (bf16[4,2,14,14,512]{4,3,2,1,0:T(8,128)(2,1)}, bf16[1,2,14,14,512]{4,3,2,1,0:T(8,128)(2,1)}, bf16[4,2,256,512]{3,2,1,0:T(8,128)(2,1)}, bf16[4,2,256...) custom-call(s32[3]{0:T(128)} %get-tuple-element.262.info, ...), custom_call_target="tpu_custom_call", output_to_operand_aliasing={{0}: (14, {}), {2}: (15, {}), {3}: (16, {}), {4}: (17, {}),... | custom-call | tf_op jit(solution)/shard_map/forward/pallas_call | solution.py:307
  137.5 4.3 collective-permute-start.1
  141.8 18.8 %backward.5 = (f32[4,2,14,14,512]{4,3,2,1,0:T(8,128)}, bf16[1,2,14,14,512]{4,3,2,1,0:T(8,128)(2,1)}, bf16[4,2,256,512]{3,2,1,0:T(8,128)(2,1)}, bf16[4,2,256,2048...) custom-call(s32[3]{0:T(128)} %get-tuple-element.263.info, ...), custom_call_target="tpu_custom_call" | custom-call | tf_op jit(solution)/shard_map/backward/pallas_call | solution.py:307
  160.7 1.5 collective-permute-start.3
  162.2 1.2 pad_add_fusion.2.info
  163.4 1.2 pad_add_fusion.6.info
  164.6 0.8 copy-done.10
  165.3 19.8 %forward.7 = (bf16[4,2,14,14,512]{4,3,2,1,0:T(8,128)(2,1)}, bf16[1,2,14,14,512]{4,3,2,1,0:T(8,128)(2,1)}, bf16[4,2,256,512]{3,2,1,0:T(8,128)(2,1)}, bf16[4,2,256...) custom-call(s32[3]{0:T(128)} %pad_add_fusion.2.info, ...), custom_call_target="tpu_custom_call", output_to_operand_aliasing={{0}: (14, {}), {2}: (15, {}), {3}: (16, {}), {4}: (17, {}),... | custom-call | tf_op jit(solution)/shard_map/forward/pallas_call | solution.py:307
  185.2 4.6 collective-permute-start.2
  190.6 18.8 %backward.6 = (f32[4,2,14,14,512]{4,3,2,1,0:T(8,128)}, bf16[1,2,14,14,512]{4,3,2,1,0:T(8,128)(2,1)}, bf16[4,2,256,512]{3,2,1,0:T(8,128)(2,1)}, bf16[4,2,256,2048...) custom-call(s32[3]{0:T(128)} %pad_add_fusion.6.info, ...), custom_call_target="tpu_custom_call", output_to_operand_aliasing={{0}: (19, {}), {2}: (20, {}), {3}: (21, {}), {4}: (22, {}),... | custom-call | tf_op jit(solution)/shard_map/backward/pallas_call | solution.py:307
  209.4 1.7 collective-permute-start.5
  211.1 1.2 pad_add_fusion.1.info
  212.2 1.2 pad_add_fusion.7.info
  213.5 0.8 copy-done.9
  214.2 19.8 %forward.8 = (bf16[4,2,14,14,512]{4,3,2,1,0:T(8,128)(2,1)}, bf16[1,2,14,14,512]{4,3,2,1,0:T(8,128)(2,1)}, bf16[4,2,256,512]{3,2,1,0:T(8,128)(2,1)}, bf16[4,2,256...) custom-call(s32[3]{0:T(128)} %pad_add_fusion.1.info, ...), custom_call_target="tpu_custom_call", output_to_operand_aliasing={{0}: (14, {}), {2}: (15, {}), {3}: (16, {}), {4}: (17, {}),... | custom-call | tf_op jit(solution)/shard_map/forward/pallas_call | solution.py:307
  234.1 4.6 collective-permute-start.4
  239.5 18.8 %backward.7 = (f32[4,2,14,14,512]{4,3,2,1,0:T(8,128)}, bf16[1,2,14,14,512]{4,3,2,1,0:T(8,128)(2,1)}, bf16[4,2,256,512]{3,2,1,0:T(8,128)(2,1)}, bf16[4,2,256,2048...) custom-call(s32[3]{0:T(128)} %pad_add_fusion.7.info, ...), custom_call_target="tpu_custom_call", output_to_operand_aliasing={{0}: (19, {}), {2}: (20, {}), {3}: (21, {}), {4}: (22, {}),... | custom-call | tf_op jit(solution)/shard_map/backward/pallas_call | solution.py:307
  258.3 1.5 collective-permute-start.6
  259.7 1.2 pad_add_fusion.info
  260.9 1.3 pad_add_fusion.9.info
  262.2 0.8 copy-done.8
  263.0 19.8 %forward.9 = (bf16[4,2,14,14,512]{4,3,2,1,0:T(8,128)(2,1)}, bf16[1,2,14,14,512]{4,3,2,1,0:T(8,128)(2,1)}, bf16[4,2,256,512]{3,2,1,0:T(8,128)(2,1)}, bf16[4,2,256...) custom-call(s32[3]{0:T(128)} %pad_add_fusion.info, ...), custom_call_target="tpu_custom_call", output_to_operand_aliasing={{0}: (14, {}), {2}: (15, {}), {3}: (16, {}), {4}: (17, {}),... | custom-call | tf_op jit(solution)/shard_map/forward/pallas_call | solution.py:307
  283.6 18.8 %backward.8 = (f32[4,2,14,14,512]{4,3,2,1,0:T(8,128)}, bf16[1,2,14,14,512]{4,3,2,1,0:T(8,128)(2,1)}, bf16[4,2,256,512]{3,2,1,0:T(8,128)(2,1)}, bf16[4,2,256,2048...) custom-call(s32[3]{0:T(128)} %pad_add_fusion.9.info, ...), custom_call_target="tpu_custom_call", output_to_operand_aliasing={{0}: (19, {}), {2}: (20, {}), {3}: (21, {}), {4}: (22, {}),... | custom-call | tf_op jit(solution)/shard_map/backward/pallas_call | solution.py:307
  302.4 1.5 collective-permute-start.7
  303.9 1.3 pad_add_fusion.8.info
  305.2 9.8 %collective-permute-done.7.returned_ref = bf16[1,2,14,14,512]{4,3,2,1,0:T(8,128)(2,1)S(1)} collective-permute-done((bf16[1,2,14,14,512]{4,3,2,1,0:T(8,128)(2,1)}, bf16[1,2,14,14,512]{4,3,2,1,0:T(8,128)(2,1)S(1)}, u32[]{:S(2)}, u32[]{:S(2)}) %collective-permute-start.7) | collective-permute-done | bytes 401440 | tf_op jit(solution)/shard_map/ppermute | solution.py:369
  315.8 19.0 %backward.9 = (f32[4,2,14,14,512]{4,3,2,1,0:T(8,128)}, bf16[1,2,14,14,512]{4,3,2,1,0:T(8,128)(2,1)}, bf16[4,2,256,512]{3,2,1,0:T(8,128)(2,1)}, bf16[4,2,256,2048...) custom-call(s32[3]{0:T(128)} %pad_add_fusion.8.info, ...), custom_call_target="tpu_custom_call", output_to_operand_aliasing={{0}: (19, {}), {2}: (20, {}), {3}: (21, {}), {4}: (22, {}),... | custom-call | tf_op jit(solution)/shard_map/backward/pallas_call | solution.py:307
  334.8 3.8 fusion.6
  338.7 7.4 %fusion = bf16[512,1536]{1,0:T(8,128)(2,1)} fusion(bf16[4,2,256,512]{3,2,1,0:T(8,128)(2,1)S(1)} %copy-done.3, bf16[4,2,256,1536]{3,2,1,0:T(8,128)(2,1)} %get-tuple-element.198), kind=kOutput, calls=%fused_computation.3 | convolution fusion | flops 3222011904 | bytes 9961472 | tf_op jit(solution)/shard_map/dot_general | solution.py:50
  346.1 9.9 %bitcast_convert_fusion.1 = bf16[512,2048]{1,0:T(8,128)(2,1)} fusion(bf16[4,2,256,512]{3,2,1,0:T(8,128)(2,1)} %get-tuple-element.200, bf16[4,2,256,2048]{3,2,1,0:T(8,128)(2,1)} %get-tuple-element.201), kind=kOutput, calls=%fused_computation.1 | convolution fusion | flops 4296015872 | bytes 12582912 | tf_op jit(solution)/shard_map/dot_general | solution.py:50
  356.3 1.3 copy-done.2
  357.6 9.5 %bitcast_convert_fusion = bf16[2048,512]{1,0:T(8,128)(2,1)} fusion(bf16[4,2,256,2048]{3,2,1,0:T(8,128)(2,1)} %get-tuple-element.202, bf16[4,2,256,512]{3,2,1,0:T(8,128)(2,1)S(1)} %copy-done.2), kind=kOutput, calls=%fused_computation | convolution fusion | flops 4296015872 | bytes 12582912 | tf_op jit(solution)/shard_map/dot_general | solution.py:50
  368.6 4.5 copy.176
  373.4 16.5 %reduce-scatter.5.cloned.1.call-done = bf16[128,1536]{1,0:T(8,128)(2,1)} async-done(((bf16[512,1536]{1,0:T(8,128)(2,1)}), bf16[128,1536]{1,0:T(8,128)(2,1)}) %reduce-scatter.5.cloned.1.call-update) | async-done | bytes 393232 | tf_op jit(solution)/shard_map/reduce_scatter | solution.py:505
  389.9 34.2 %reduce-scatter.9.cloned.1.call-done = bf16[128,2048]{1,0:T(8,128)(2,1)} async-done(((bf16[512,2048]{1,0:T(8,128)(2,1)}), bf16[128,2048]{1,0:T(8,128)(2,1)}) %reduce-scatter.9.cloned.1.call-update) | async-done | bytes 524304 | tf_op jit(solution)/shard_map/reduce_scatter | solution.py:505
  424.1 33.7 %reduce-scatter.11.cloned.1.call-done = bf16[512,512]{1,0:T(8,128)(2,1)} async-done(((bf16[2048,512]{1,0:T(8,128)(2,1)}), bf16[512,512]{1,0:T(8,128)(2,1)}) %reduce-scatter.11.cloned.1.call-update) | async-done | bytes 524304 | tf_op jit(solution)/shard_map/reduce_scatter | solution.py:505
  458.3 1.0 fusion.8
  459.7 10.6 %all-reduce.4 = f32[4,3072]{1,0:T(4,128)S(1)} all-reduce(f32[4,3072]{1,0:T(4,128)S(1)} %select_maximum_fusion), channel_id=10, replica_groups=mesh['section'=2,'fsdp'=4,'replica'=4] {'fsdp'}, use_global_device_ids=true, to_apply=%region_10.11.clone | all-reduce | flops 12288 | bytes 98304
  471.0 20.4 %psum.39 = f32[1,3072]{1,0:T(1,128)S(1)} all-reduce(f32[1,3072]{1,0:T(1,128)S(1)} %constant_dynamic-slice_fusion.10), channel_id=1, replica_groups=mesh['section'=2,'fsdp'=4,'replica'=4] {'replica'}, use_global_device_ids=true, to_apply=%region_11.12 | all-reduce | flops 3072 | bytes 24576 | tf_op jit(solution)/shard_map/psum | solution.py:518
  492.5 6.7 %copy.177 = f32[1,4,2,14,14,512]{5,2,4,3,1,0:T(2,128)} copy(f32[1,4,2,14,14,512]{5,4,3,2,1,0:T(8,128)} %bitcast.147) | data formatting | bytes 6422528
  500.6 29.5 %all-reduce.8.cloned.1.call-done = (bf16[1,128,1536]{2,1,0:T(8,128)(2,1)}, bf16[1,128,512]{2,1,0:T(8,128)(2,1)}, bf16[1,128,2048]{2,1,0:T(8,128)(2,1)}, bf16[1,512,512]{2,1,0:T(8,128)(2,1)}) async-done(((bf16[1,128,1536]{2,1,0:T(8,128)(2,1)}, bf16[1,128,512]{2,1,0:T(8,128)(2,1)}, bf16[1,128,2048]{2,1,0:T(8,128)(2,1)}, bf16[1,512,512]{2,1,0:T(8,128)(2,1)}), (bf16[1,128,1536]{2,1,0:T(8,128)(2,1)}, ...) | async-done | bytes 1572880 | tf_op jit(solution)/shard_map/psum | solution.py:506
  530.1 2.0 broadcast_in_dim.65
  532.1 1.6 broadcast_in_dim.67
  533.7 2.1 broadcast_in_dim.69
  535.9 1.1 broadcast_in_dim.71
  (123 shorter events, 16.8 us)
Async XLA Ops:
  7.2 3.3 copy-start.5
  7.2 32.3 %all-gather.8.cloned.1.call-start = ((), (), s32[]{:S(2)}) async-start(), calls=%async_computation.8 | async-start | bytes 1966080 | tf_op jit(solution)/shard_map/all_gather | solution.py:399
  7.9 50.1 %all-gather.10.cloned.1.call-start = ((), (), s32[]{:S(2)}) async-start(), calls=%async_computation.9 | async-start | bytes 2621440 | tf_op jit(solution)/shard_map/all_gather | solution.py:401
  8.7 73.5 %all-gather.12.cloned.1.call-start = ((), (), s32[]{:S(2)}) async-start(), calls=%async_computation.10 | async-start | bytes 2621440 | tf_op jit(solution)/shard_map/all_gather | solution.py:402
  9.4 364.0 %reduce-scatter.7.cloned.1.call-start = ((), (), s32[]{:S(2)}) async-start(), calls=%async_computation.5 | async-start | bytes 655360 | tf_op jit(solution)/shard_map/reduce_scatter | solution.py:505
  12.3 0.7 copy-start.20
  12.3 1.0 copy-start.21
  12.3 1.0 copy-start.22
  12.3 1.0 copy-start.23
  12.3 7.6 %copy-start.18 = (s32[49,49]{1,0:T(8,128)S(1)}, s32[49,49]{1,0:T(8,128)}, u32[]{:S(2)}) copy-start(s32[49,49]{1,0:T(8,128)} %param.17) | copy-start | bytes 28816
  12.9 9.2 %copy-start.17 = (s32[4,1]{0,1:T(1,128)S(1)}, s32[4,1]{0,1:T(1,128)}, u32[]{:S(2)}) copy-start(s32[4,1]{0,1:T(1,128)} %param.15) | copy-start | bytes 52
  13.0 11.3 %copy-start.16 = (bf16[1,128,512]{2,1,0:T(8,128)(2,1)S(1)}, bf16[1,128,512]{2,1,0:T(8,128)(2,1)}, u32[]{:S(2)}) copy-start(bf16[1,128,512]{2,1,0:T(8,128)(2,1)} %param.19) | copy-start | bytes 393220
  83.0 23.6 %copy-start.6 = (bf16[4,2,14,14,512]{4,1,3,2,0:T(2,128)(2,1)S(1)}, bf16[4,2,14,14,512]{4,1,3,2,0:T(2,128)(2,1)}, u32[]{:S(2)}) copy-start(bf16[4,2,14,14,512]{4,1,3,2,0:T(2,128)(2,1)} %param.14) | copy-start | bytes 4816900
  103.0 13.9 %collective-permute-start = (bf16[1,2,14,14,512]{4,3,2,1,0:T(8,128)(2,1)}, bf16[1,2,14,14,512]{4,3,2,1,0:T(8,128)(2,1)S(1)}, u32[]{:S(2)}, u32[]{:S(2)}) collective-permute-start(bf16[1,2,14,14,512]{4,3,2,1,0:T(8,128)(2,1)} %get-tuple-element.108), channel_id=1, source_target_pairs={{0,16},{1,17},{2,18},{3,19},{4,20},{5,21},{6,22},{7,23},{8,24},{9,... | collective-permute-start | bytes 1204232 | tf_op jit(solution)/shard_map/ppermute | solution.py:369
  116.9 0.8 copy-start.11
  137.5 27.1 %collective-permute-start.1 = (bf16[1,2,14,14,512]{4,3,2,1,0:T(8,128)(2,1)}, bf16[1,2,14,14,512]{4,3,2,1,0:T(8,128)(2,1)S(1)}, u32[]{:S(2)}, u32[]{:S(2)}) collective-permute-start(bf16[1,2,14,14,512]{4,3,2,1,0:T(8,128)(2,1)} %get-tuple-element.120), channel_id=1, source_target_pairs={{0,16},{1,17},{2,18},{3,19},{4,20},{5,21},{6,22},{7,23},{8,24},{9,... | collective-permute-start | bytes 1204232 | tf_op jit(solution)/shard_map/ppermute | solution.py:369
  160.7 29.1 %collective-permute-start.3 = (bf16[1,2,14,14,512]{4,3,2,1,0:T(8,128)(2,1)}, bf16[1,2,14,14,512]{4,3,2,1,0:T(8,128)(2,1)S(1)}, u32[]{:S(2)}, u32[]{:S(2)}) collective-permute-start(bf16[1,2,14,14,512]{4,3,2,1,0:T(8,128)(2,1)} %get-tuple-element.145), channel_id=1, source_target_pairs={{16,0},{17,1},{18,2},{19,3},{20,4},{21,5},{22,6},{23,7},{24,8},{25... | collective-permute-start | bytes 1204232 | tf_op jit(solution)/shard_map/ppermute | solution.py:369
  164.6 0.8 copy-start.10
  185.2 28.3 %collective-permute-start.2 = (bf16[1,2,14,14,512]{4,3,2,1,0:T(8,128)(2,1)}, bf16[1,2,14,14,512]{4,3,2,1,0:T(8,128)(2,1)S(1)}, u32[]{:S(2)}, u32[]{:S(2)}) collective-permute-start(bf16[1,2,14,14,512]{4,3,2,1,0:T(8,128)(2,1)} %get-tuple-element.133), channel_id=1, source_target_pairs={{0,16},{1,17},{2,18},{3,19},{4,20},{5,21},{6,22},{7,23},{8,24},{9,... | collective-permute-start | bytes 1204232 | tf_op jit(solution)/shard_map/ppermute | solution.py:369
  189.8 0.8 copy-start.13
  209.4 29.3 %collective-permute-start.5 = (bf16[1,2,14,14,512]{4,3,2,1,0:T(8,128)(2,1)}, bf16[1,2,14,14,512]{4,3,2,1,0:T(8,128)(2,1)S(1)}, u32[]{:S(2)}, u32[]{:S(2)}) collective-permute-start(bf16[1,2,14,14,512]{4,3,2,1,0:T(8,128)(2,1)} %get-tuple-element.165), channel_id=1, source_target_pairs={{16,0},{17,1},{18,2},{19,3},{20,4},{21,5},{22,6},{23,7},{24,8},{25... | collective-permute-start | bytes 1204232 | tf_op jit(solution)/shard_map/ppermute | solution.py:369
  213.5 0.8 copy-start.9
  234.1 28.1 %collective-permute-start.4 = (bf16[1,2,14,14,512]{4,3,2,1,0:T(8,128)(2,1)}, bf16[1,2,14,14,512]{4,3,2,1,0:T(8,128)(2,1)S(1)}, u32[]{:S(2)}, u32[]{:S(2)}) collective-permute-start(bf16[1,2,14,14,512]{4,3,2,1,0:T(8,128)(2,1)} %get-tuple-element.153), channel_id=1, source_target_pairs={{0,16},{1,17},{2,18},{3,19},{4,20},{5,21},{6,22},{7,23},{8,24},{9,... | collective-permute-start | bytes 1204232 | tf_op jit(solution)/shard_map/ppermute | solution.py:369
  238.7 0.8 copy-start.14
  258.3 24.5 %collective-permute-start.6 = (bf16[1,2,14,14,512]{4,3,2,1,0:T(8,128)(2,1)}, bf16[1,2,14,14,512]{4,3,2,1,0:T(8,128)(2,1)S(1)}, u32[]{:S(2)}, u32[]{:S(2)}) collective-permute-start(bf16[1,2,14,14,512]{4,3,2,1,0:T(8,128)(2,1)} %get-tuple-element.174), channel_id=1, source_target_pairs={{16,0},{17,1},{18,2},{19,3},{20,4},{21,5},{22,6},{23,7},{24,8},{25... | collective-permute-start | bytes 1204232 | tf_op jit(solution)/shard_map/ppermute | solution.py:369
  262.2 0.8 copy-start.8
  282.8 0.8 copy-start.12
  302.4 12.6 %collective-permute-start.7 = (bf16[1,2,14,14,512]{4,3,2,1,0:T(8,128)(2,1)}, bf16[1,2,14,14,512]{4,3,2,1,0:T(8,128)(2,1)S(1)}, u32[]{:S(2)}, u32[]{:S(2)}) collective-permute-start(bf16[1,2,14,14,512]{4,3,2,1,0:T(8,128)(2,1)} %get-tuple-element.188), channel_id=1, source_target_pairs={{16,0},{17,1},{18,2},{19,3},{20,4},{21,5},{22,6},{23,7},{24,8},{25... | collective-permute-start | bytes 1204232 | tf_op jit(solution)/shard_map/ppermute | solution.py:369
  315.0 0.8 copy-start.15
  315.8 19.0 %copy-start = (bf16[4,2,256,512]{3,2,1,0:T(8,128)(2,1)S(1)}, bf16[4,2,256,512]{3,2,1,0:T(8,128)(2,1)}, u32[]{:S(2)}) copy-start(bf16[4,2,256,512]{3,2,1,0:T(8,128)(2,1)} %get-tuple-element.179.o_ref) | copy-start | bytes 6291460
  334.8 3.9 copy-start.3
  338.6 51.3 %reduce-scatter.5.cloned.1.call-start = ((), (), s32[]{:S(2)}) async-start(), calls=%async_computation.4 | async-start | bytes 1966080 | tf_op jit(solution)/shard_map/reduce_scatter | solution.py:505
  346.1 78.0 %reduce-scatter.9.cloned.1.call-start = ((), (), s32[]{:S(2)}) async-start(), calls=%async_computation.6 | async-start | bytes 2621440 | tf_op jit(solution)/shard_map/reduce_scatter | solution.py:505
  356.0 1.6 copy-start.2
  356.0 101.8 %reduce-scatter.11.cloned.1.call-start = ((), (), s32[]{:S(2)}) async-start(), calls=%async_computation.7 | async-start | bytes 2621440 | tf_op jit(solution)/shard_map/reduce_scatter | solution.py:505
  367.1 0.7 copy-start.19
  367.1 0.9 copy-start.24
  367.2 5.9 %copy-start.1 = (f32[4,2,64,1024]{3,2,1,0:T(8,128)S(1)}, f32[4,2,64,1024]{3,2,1,0:T(8,128)}, u32[]{:S(2)}) copy-start(f32[4,2,64,1024]{3,2,1,0:T(8,128)} %get-tuple-element.205) | copy-start | bytes 6291460
  367.2 162.9 %all-reduce.8.cloned.1.call-start = ((), (), s32[]{:S(2)}) async-start(), calls=%async_computation.11 | async-start | bytes 3145728 | tf_op jit(solution)/shard_map/psum | solution.py:506
  457.8 1.8 copy-start.4
  530.1 5.8 %copy-start.7 = (bf16[1,512,512]{2,1,0:T(8,128)(2,1)S(1)}, bf16[1,512,512]{2,1,0:T(8,128)(2,1)}, u32[]{:S(2)}) copy-start(bf16[1,512,512]{2,1,0:T(8,128)(2,1)} %get-tuple-element.249) | copy-start | bytes 1572868
Sparse Core Ops, SparseCore 0:
  9.6 24.7 all-gather.7
  35.9 22.0 all-gather.9
  59.6 22.5 all-gather.11
  338.7 20.7 reduce-scatter.6
  361.9 27.9 reduce-scatter.4
  392.9 31.1 reduce-scatter.8
  426.6 31.1 reduce-scatter.10
  460.4 69.6 all-reduce.7
